TPU v7x, 256 devices: a whole 4x4x8 slice. The times are simulated.
256 devices in a mesh: sector: 8 (over x, core), section: 32 (over z, y).
Axes of the slice: x: 4, y: 4, z: 8, core: 2. Of those that a mesh axis runs over, the one named last changes fastest.
Arguments:
- vectors: bfloat16 [98304, 512], P(('sector', 'section')), may hold values from -6 to 6
- sectors: int32 [98304, 2], P(('sector', 'section')), may hold values from 0 to 31, all different within a row; in each aligned block of 384 rows (0 to 383, 384 to 767, ...) at most 36 rows name the same one
- outcomes: int32 [98304, 2], P(('sector', 'section')), may hold values from 0 to 3
- sites: bfloat16 [2, 32, 512, 2048], P(None, 'sector'), may hold values from -0.25 to 0.25
- environments: bfloat16 [2, 32, 4, 512, 512], P(None, 'sector', None, 'section'), may hold values from -100 to 150, as said below
Outputs:
- probabilities: bfloat16 [98304, 8], P(('sector', 'section'))
- final_vectors: bfloat16 [98304, 512], P(('sector', 'section'))
Inputs may be any that keep to these rules, and one draw needn't show every extreme that they name: `sectors`: in the rows of one device no sector appears more than 36 times over all orbitals together, and on some device some sector appears exactly 36 times. Every block environments[k, q, s] is symmetric and positive definite.
All inputs are finite; a program needn't handle non-finite values.
Results may differ from a plain program's by a relative error of at most 0.0049.
Values may be sent and summed in bfloat16 or wider, within the bound.
No kernel may reach another device: no remote copies, remote signals or barrier semaphores. Data moves between devices by JAX's collectives and lax.ppermute only.
A program may use at most 128 MiB of HBM per device.

v0:
```python
import jax
import jax.numpy as jnp
from jax import lax
from jax.sharding import PartitionSpec as P

OUTCOMES = 4
ORBITALS = 2


def slot_positions(labels, sector_total):
    onehot = (labels[:, None] == jnp.arange(sector_total, dtype=jnp.int32)[None, :]).astype(
        jnp.int32
    )
    before = jnp.cumsum(onehot, axis=0) - onehot
    return jnp.sum(before * onehot, axis=1)


def branch_results(amplitudes, images, id_grid, block_width):
    weights = jnp.sum(images * amplitudes, axis=-1)
    norm_sum = jnp.sum(weights, axis=-1)
    filled = id_grid >= 0.0
    branch_probs = (weights / jnp.where(filled, norm_sum, 1.0)[..., None]).astype(jnp.bfloat16)
    chosen_mask = (id_grid[..., None] == jnp.arange(OUTCOMES, dtype=jnp.float32)).astype(
        jnp.float32
    )
    chosen_weight = jnp.sum(chosen_mask * weights, axis=-1)
    picked = jnp.sum(chosen_mask[..., None] * amplitudes, axis=-2)
    rescale = lax.rsqrt(jnp.where(filled, chosen_weight, 1.0) / block_width)
    advanced = (picked * rescale[..., None]).astype(jnp.bfloat16)
    return (branch_probs, advanced)


def local(vectors, sectors, outcomes, sites, environments):
    sector_count = lax.axis_size("sector")
    per_device = sites.shape[1]
    sector_total = per_device * sector_count
    sample_count = vectors.shape[0]
    block_width = vectors.shape[1]
    capacity = max(2, (3 * sample_count + sector_total - 1) // sector_total)
    current = vectors
    columns = []
    for orbital in range(ORBITALS):
        environ_k = lax.all_gather(environments[orbital], "section", axis=2, tiled=True)
        site_k = sites[orbital]
        labels = sectors[:, orbital]
        slot_of = labels * capacity + slot_positions(labels, sector_total)
        send_rows = (
            jnp.zeros((sector_total * capacity, block_width), jnp.bfloat16).at[slot_of].set(current)
        )
        send_rows = send_rows.reshape(sector_total, capacity, block_width)
        send_ids = (
            jnp.full((sector_total * capacity,), -1.0, jnp.bfloat16)
            .at[slot_of]
            .set(outcomes[:, orbital].astype(jnp.bfloat16))
        )
        send_ids = send_ids.reshape(sector_total, capacity)
        rows_in = lax.all_to_all(send_rows, "sector", split_axis=0, concat_axis=0, tiled=True)
        ids_in = lax.all_to_all(send_ids, "sector", split_axis=0, concat_axis=0, tiled=True)
        slot_count = rows_in.shape[1]
        arranged = rows_in.reshape(sector_count, per_device, slot_count, block_width)
        amplitudes = jnp.einsum(
            "iqcb,qbf->iqcf", arranged, site_k, preferred_element_type=jnp.float32
        )
        amplitudes = amplitudes.reshape(sector_count, per_device, slot_count, OUTCOMES, block_width)
        rounded = amplitudes.astype(jnp.bfloat16)
        images = jnp.einsum(
            "iqcsb,qsbe->iqcse", rounded, environ_k, preferred_element_type=jnp.float32
        )
        id_grid = ids_in.astype(jnp.float32).reshape(sector_count, per_device, slot_count)
        branch_probs, advanced = branch_results(amplitudes, images, id_grid, block_width)
        probs_back, rows_back = (
            lax.all_to_all(
                branch_probs.reshape(sector_total, slot_count, OUTCOMES),
                "sector",
                split_axis=0,
                concat_axis=0,
                tiled=True,
            ),
            lax.all_to_all(
                advanced.reshape(sector_total, slot_count, block_width),
                "sector",
                split_axis=0,
                concat_axis=0,
                tiled=True,
            ),
        )
        columns.append(probs_back.reshape(sector_total * capacity, OUTCOMES)[slot_of])
        current = rows_back.reshape(sector_total * capacity, block_width)[slot_of]
    return (jnp.concatenate(columns, axis=1), current)


def solution(mesh):
    placed = (
        P(("sector", "section"), None),
        P(("sector", "section"), None),
        P(("sector", "section"), None),
        P(None, "sector", None, None),
        P(None, "sector", None, "section", None),
    )
    return jax.shard_map(
        local,
        mesh=mesh,
        in_specs=placed,
        out_specs=(P(("sector", "section"), None), P(("sector", "section"), None)),
        check_vma=False,
    )
```

profile of v0, /device:TPU:1, one launch (start us, length us, event | category | flops | bytes accessed | tf_op | source)
XLA Modules:
  0.0 290.2 jit_solution(226082622245741807)
XLA Ops:
  7.2 1.8 fusion.45
  13.3 3.0 %scatter_custom_fusion.1 = bf16[1152]{0:T(1024)(128)(2,1)S(1)} fusion(s32[384]{0:T(512)S(1)} %get-tuple-element.10, bf16[384]{0:T(512)(128)(2,1)S(1)} %get-tuple-element.13, bf16[]{:T(256)} %constant.25.clone.1), kind=kCustom, calls=%fused_computation.82 | custom fusion | bytes 2306 | tf_op jit(solution)/shard_map/scatter | solution.py:54
  17.0 6.4 %all-to-all-start.1 = ((bf16[8,4,36]{2,1,0:T(4,128)(2,1)}), bf16[8,4,36]{2,1,0:T(4,128)(2,1)S(1)}, u32[]{:S(2)}, u32[]{:S(2)}) async-start(bf16[8,4,36]{2,1,0:T(4,128)(2,1)} %all_to_all.31), calls=%async_computation.1 | async-start | bytes 16384 | tf_op jit(solution)/shard_map/all_to_all | solution.py:58
  23.4 2.8 scatter_custom_fusion
  28.0 4.8 %all-to-all-start = ((bf16[32,36,512]{2,1,0:T(8,128)(2,1)}), bf16[32,36,512]{2,1,0:T(8,128)(2,1)S(1)}, u32[]{:S(2)}, u32[]{:S(2)}) async-start(bf16[32,36,512]{2,1,0:T(8,128)(2,1)} %reshape.115), calls=%async_computation | async-start | bytes 2621440 | tf_op jit(solution)/shard_map/all_to_all | solution.py:57
  33.2 17.5 %all-to-all-done = bf16[32,36,512]{2,1,0:T(8,128)(2,1)S(1)} async-done(((bf16[32,36,512]{2,1,0:T(8,128)(2,1)}), bf16[32,36,512]{2,1,0:T(8,128)(2,1)S(1)}, u32[]{:S(2)}, u32[]{:S(2)}) %all-to-all-start) | async-done | bytes 1179680 | tf_op jit(solution)/shard_map/all_to_all | solution.py:57
  50.7 10.3 %fusion.12 = f32[8,4,36,2048]{3,2,0,1:T(8,128)} fusion(bf16[2,4,512,2048]{3,2,1,0:T(8,128)(2,1)} %param.8, bf16[8,4,36,512]{3,2,1,0:T(8,128)(2,1)S(1)} %bitcast.119), kind=kOutput, calls=%fused_computation.26 | convolution fusion | flops 2415919104 | bytes 19005440 | tf_op jit(solution)/shard_map/iqcb,qbf->iqcf/dot_general | solution.py:61
  60.9 12.0 %reshape.196 = f32[8,4,36,4,512]{4,3,2,0,1:T(4,128)} reshape(f32[8,4,36,2048]{3,2,0,1:T(8,128)} %fusion.12) | data formatting | bytes 18874368 | tf_op jit(solution)/shard_map/reshape | solution.py:64
  73.0 8.0 %multiply_reduce_fusion.1 = f32[8,4,36,512]{3,0,2,1:T(8,128)S(1)} fusion(f32[8,4,36,4,512]{4,3,2,0,1:T(4,128)} %reshape.196, f32[8,4,36,4]{3,0,2,1:T(8,128)S(1)} %copy.116), kind=kLoop, calls=%fused_computation.11 | loop fusion | flops 4128768 | bytes 11814912 | tf_op jit(solution)/shard_map/reduce_sum | solution.py:27
  81.0 3.5 %copy.117 = f32[8,4,36,512]{3,1,0,2:T(4,128)} copy(f32[8,4,36,512]{3,0,2,1:T(8,128)S(1)} %multiply_reduce_fusion.1) | data formatting | bytes 4718592 | tf_op jit(solution)/shard_map/reduce_sum | solution.py:27
  84.5 2.7 reduce_sum.110
  87.2 25.2 %all-gather.5.cloned.1.call-done = bf16[1,4,4,512,512]{4,3,2,1,0:T(8,128)(2,1)} async-done(((bf16[1,4,4,16,512]{4,3,2,1,0:T(8,128)(2,1)}), bf16[1,4,4,512,512]{4,3,2,1,0:T(8,128)(2,1)}) %all-gather.5.cloned.1.call-update) | async-done | bytes 8388624 | tf_op jit(solution)/shard_map/all_gather | solution.py:43
  112.3 19.2 %fusion.18 = (f32[8,4,36]{2,0,1:T(8,128)S(1)}, f32[8,4,36,4]{2,0,3,1:T(8,128)S(1)}) fusion(f32[8,4,36,4,512]{4,3,2,0,1:T(4,128)} %reshape.196, bf16[1,4,4,512,512]{4,3,2,1,0:T(8,128)(2,1)} %all-gather.5.cloned.1.call-done), kind=kOutput, calls=%fused_computation.28 | convolution fusion | flops 2422991360 | bytes 17848832 | tf_op jit(solution)/shard_map/iqcsb,qsbe->iqcse/dot_general | solution.py:66
  133.7 5.3 %all-to-all-start.3 = ((bf16[32,36,512]{2,1,0:T(8,128)(2,1)}), bf16[32,36,512]{2,1,0:T(8,128)(2,1)S(1)}, u32[]{:S(2)}, u32[]{:S(2)}) async-start(bf16[32,36,512]{2,1,0:T(8,128)(2,1)} %copy.122), calls=%async_computation.3 | async-start | bytes 2621440 | tf_op jit(solution)/shard_map/all_to_all | solution.py:79
  140.3 3.0 %scatter_custom_fusion.3 = bf16[1152]{0:T(1024)(128)(2,1)S(1)} fusion(s32[384]{0:T(512)S(1)} %fusion.44, bf16[384]{0:T(512)(128)(2,1)S(1)} %get-tuple-element.12, bf16[]{:T(256)} %constant.25.clone.1), kind=kCustom, calls=%fused_computation.80 | custom fusion | bytes 2306 | tf_op jit(solution)/shard_map/scatter | solution.py:54
  144.0 12.9 %all-to-all-done.3 = bf16[32,36,512]{2,1,0:T(8,128)(2,1)S(1)} async-done(((bf16[32,36,512]{2,1,0:T(8,128)(2,1)}), bf16[32,36,512]{2,1,0:T(8,128)(2,1)S(1)}, u32[]{:S(2)}, u32[]{:S(2)}) %all-to-all-start.3) | async-done | bytes 1179680 | tf_op jit(solution)/shard_map/all_to_all | solution.py:79
  156.9 4.1 %all-to-all-start.5 = ((bf16[8,4,36]{2,1,0:T(4,128)(2,1)}), bf16[8,4,36]{2,1,0:T(4,128)(2,1)S(1)}, u32[]{:S(2)}, u32[]{:S(2)}) async-start(bf16[8,4,36]{2,1,0:T(4,128)(2,1)} %all_to_all.36), calls=%async_computation.5 | async-start | bytes 16384 | tf_op jit(solution)/shard_map/all_to_all | solution.py:58
  161.3 4.1 %scatter_custom_fusion.2 = bf16[1152,512]{1,0:T(8,128)(2,1)S(1)} fusion(s32[384]{0:T(512)S(1)} %fusion.44, bf16[]{:T(256)} %constant.9.clone.1, bf16[1152,512]{1,0:T(8,128)(2,1)S(1)} %reshape.120, s32[1024]{0:T(1024)S(1)} %pad_clamp_fusion.1), kind=kCustom, calls=%fused_computation.36 | custom fusion | bytes 1179650 | tf_op jit(solution)/shard_map/scatter | solution.py:48
  166.6 4.8 %all-to-all-start.4 = ((bf16[32,36,512]{2,1,0:T(8,128)(2,1)}), bf16[32,36,512]{2,1,0:T(8,128)(2,1)S(1)}, u32[]{:S(2)}, u32[]{:S(2)}) async-start(bf16[32,36,512]{2,1,0:T(8,128)(2,1)} %reshape.121), calls=%async_computation.4 | async-start | bytes 2621440 | tf_op jit(solution)/shard_map/all_to_all | solution.py:57
  172.6 16.7 %all-to-all-done.4 = bf16[32,36,512]{2,1,0:T(8,128)(2,1)S(1)} async-done(((bf16[32,36,512]{2,1,0:T(8,128)(2,1)}), bf16[32,36,512]{2,1,0:T(8,128)(2,1)S(1)}, u32[]{:S(2)}, u32[]{:S(2)}) %all-to-all-start.4) | async-done | bytes 1179680 | tf_op jit(solution)/shard_map/all_to_all | solution.py:57
  189.3 4.3 %all-to-all-start.2 = ((bf16[8,2,288]{2,1,0:T(2,128)(2,1)}), bf16[8,2,288]{2,1,0:T(2,128)(2,1)S(1)}, u32[]{:S(2)}, u32[]{:S(2)}) async-start(bf16[8,2,288]{2,1,0:T(2,128)(2,1)} %reshape.222), calls=%async_computation.2 | async-start | bytes 24576 | tf_op jit(solution)/shard_map/all_to_all | solution.py:72
  193.6 10.3 %fusion.15 = f32[8,4,36,2048]{3,2,0,1:T(8,128)} fusion(bf16[2,4,512,2048]{3,2,1,0:T(8,128)(2,1)} %param.8, bf16[8,4,36,512]{3,2,1,0:T(8,128)(2,1)S(1)} %bitcast.118), kind=kOutput, calls=%fused_computation.27 | convolution fusion | flops 2415919104 | bytes 19005440 | tf_op jit(solution)/shard_map/iqcb,qbf->iqcf/dot_general | solution.py:61
  204.0 11.9 %reshape.197 = f32[8,4,36,4,512]{4,3,2,0,1:T(4,128)} reshape(f32[8,4,36,2048]{3,2,0,1:T(8,128)} %fusion.15) | data formatting | bytes 18874368 | tf_op jit(solution)/shard_map/reshape | solution.py:64
  215.9 19.1 %fusion.20 = (f32[8,4,36]{2,0,1:T(8,128)S(1)}, f32[8,4,36,4]{2,0,3,1:T(8,128)S(1)}) fusion(f32[8,4,36,4,512]{4,3,2,0,1:T(4,128)} %reshape.197, bf16[1,4,4,512,512]{4,3,2,1,0:T(8,128)(2,1)} %all-gather.7.cloned.1.call-done), kind=kOutput, calls=%fused_computation.30 | convolution fusion | flops 2422991360 | bytes 17848832 | tf_op jit(solution)/shard_map/iqcsb,qsbe->iqcse/dot_general | solution.py:66
  235.0 6.4 %multiply_reduce_fusion = f32[8,4,36,512]{3,0,2,1:T(8,128)S(1)} fusion(f32[8,4,36,4,512]{4,3,2,0,1:T(4,128)S(1)} %copy-done, f32[8,4,36,4]{3,0,2,1:T(8,128)S(1)} %copy.136), kind=kLoop, calls=%fused_computation.10 | loop fusion | flops 4128768 | bytes 11814912 | tf_op jit(solution)/shard_map/reduce_sum | solution.py:27
  241.6 3.5 %copy.137 = f32[8,4,36,512]{3,1,0,2:T(4,128)} copy(f32[8,4,36,512]{3,0,2,1:T(8,128)S(1)} %multiply_reduce_fusion) | data formatting | bytes 4718592 | tf_op jit(solution)/shard_map/reduce_sum | solution.py:27
  245.0 2.7 reduce_sum.116
  248.5 4.8 %all-to-all-start.6 = ((bf16[8,2,288]{2,1,0:T(2,128)(2,1)}), bf16[8,2,288]{2,1,0:T(2,128)(2,1)S(1)}, u32[]{:S(2)}, u32[]{:S(2)}) async-start(bf16[8,2,288]{2,1,0:T(2,128)(2,1)} %reshape.220), calls=%async_computation.6 | async-start | bytes 24576 | tf_op jit(solution)/shard_map/all_to_all | solution.py:72
  255.2 2.7 all-to-all-done.6
  257.9 4.2 %all-to-all-start.7 = ((bf16[32,36,512]{2,1,0:T(8,128)(2,1)}), bf16[32,36,512]{2,1,0:T(8,128)(2,1)S(1)}, u32[]{:S(2)}, u32[]{:S(2)}) async-start(bf16[32,36,512]{2,1,0:T(8,128)(2,1)} %copy.142), calls=%async_computation.7 | async-start | bytes 2621440 | tf_op jit(solution)/shard_map/all_to_all | solution.py:79
  266.8 13.2 %all-to-all-done.7 = bf16[32,36,512]{2,1,0:T(8,128)(2,1)S(1)} async-done(((bf16[32,36,512]{2,1,0:T(8,128)(2,1)}), bf16[32,36,512]{2,1,0:T(8,128)(2,1)S(1)}, u32[]{:S(2)}, u32[]{:S(2)}) %all-to-all-start.7) | async-done | bytes 1179680 | tf_op jit(solution)/shard_map/all_to_all | solution.py:79
  280.3 2.6 gather_fusion.2
  (76 shorter events, 21.6 us)
Async XLA Ops:
  7.2 105.2 %all-gather.5.cloned.1.call-start = ((), (), s32[]{:S(2)}) async-start(), calls=%async_computation.8 | async-start | bytes 8650752 | tf_op jit(solution)/shard_map/all_gather | solution.py:43
  9.1 206.8 %all-gather.7.cloned.1.call-start = ((), (), s32[]{:S(2)}) async-start(), calls=%async_computation.9 | async-start | bytes 8650752 | tf_op jit(solution)/shard_map/all_gather | solution.py:43
  17.0 11.1 %all-to-all-start.1 = ((bf16[8,4,36]{2,1,0:T(4,128)(2,1)}), bf16[8,4,36]{2,1,0:T(4,128)(2,1)S(1)}, u32[]{:S(2)}, u32[]{:S(2)}) async-start(bf16[8,4,36]{2,1,0:T(4,128)(2,1)} %all_to_all.31), calls=%async_computation.1 | async-start | bytes 16384 | tf_op jit(solution)/shard_map/all_to_all | solution.py:58
  28.0 22.6 %all-to-all-start = ((bf16[32,36,512]{2,1,0:T(8,128)(2,1)}), bf16[32,36,512]{2,1,0:T(8,128)(2,1)S(1)}, u32[]{:S(2)}, u32[]{:S(2)}) async-start(bf16[32,36,512]{2,1,0:T(8,128)(2,1)} %reshape.115), calls=%async_computation | async-start | bytes 2621440 | tf_op jit(solution)/shard_map/all_to_all | solution.py:57
  131.9 8.3 %copy-start.1 = (s32[384,2]{0,1:T(2,128)S(1)}, s32[384,2]{0,1:T(2,128)}, u32[]{:S(2)}) copy-start(s32[384,2]{0,1:T(2,128)} %param.6) | copy-start | bytes 9220
  133.7 23.2 %all-to-all-start.3 = ((bf16[32,36,512]{2,1,0:T(8,128)(2,1)}), bf16[32,36,512]{2,1,0:T(8,128)(2,1)S(1)}, u32[]{:S(2)}, u32[]{:S(2)}) async-start(bf16[32,36,512]{2,1,0:T(8,128)(2,1)} %copy.122), calls=%async_computation.3 | async-start | bytes 2621440 | tf_op jit(solution)/shard_map/all_to_all | solution.py:79
  156.9 9.6 %all-to-all-start.5 = ((bf16[8,4,36]{2,1,0:T(4,128)(2,1)}), bf16[8,4,36]{2,1,0:T(4,128)(2,1)S(1)}, u32[]{:S(2)}, u32[]{:S(2)}) async-start(bf16[8,4,36]{2,1,0:T(4,128)(2,1)} %all_to_all.36), calls=%async_computation.5 | async-start | bytes 16384 | tf_op jit(solution)/shard_map/all_to_all | solution.py:58
  166.6 22.7 %all-to-all-start.4 = ((bf16[32,36,512]{2,1,0:T(8,128)(2,1)}), bf16[32,36,512]{2,1,0:T(8,128)(2,1)S(1)}, u32[]{:S(2)}, u32[]{:S(2)}) async-start(bf16[32,36,512]{2,1,0:T(8,128)(2,1)} %reshape.121), calls=%async_computation.4 | async-start | bytes 2621440 | tf_op jit(solution)/shard_map/all_to_all | solution.py:57
  189.3 59.2 %all-to-all-start.2 = ((bf16[8,2,288]{2,1,0:T(2,128)(2,1)}), bf16[8,2,288]{2,1,0:T(2,128)(2,1)S(1)}, u32[]{:S(2)}, u32[]{:S(2)}) async-start(bf16[8,2,288]{2,1,0:T(2,128)(2,1)} %reshape.222), calls=%async_computation.2 | async-start | bytes 24576 | tf_op jit(solution)/shard_map/all_to_all | solution.py:72
  215.9 19.2 %copy-start = (f32[8,4,36,4,512]{4,3,2,0,1:T(4,128)S(1)}, f32[8,4,36,4,512]{4,3,2,0,1:T(4,128)}, u32[]{:S(2)}) copy-start(f32[8,4,36,4,512]{4,3,2,0,1:T(4,128)} %reshape.197) | copy-start | bytes 28311556
  248.5 9.5 %all-to-all-start.6 = ((bf16[8,2,288]{2,1,0:T(2,128)(2,1)}), bf16[8,2,288]{2,1,0:T(2,128)(2,1)S(1)}, u32[]{:S(2)}, u32[]{:S(2)}) async-start(bf16[8,2,288]{2,1,0:T(2,128)(2,1)} %reshape.220), calls=%async_computation.6 | async-start | bytes 24576 | tf_op jit(solution)/shard_map/all_to_all | solution.py:72
  257.9 22.1 %all-to-all-start.7 = ((bf16[32,36,512]{2,1,0:T(8,128)(2,1)}), bf16[32,36,512]{2,1,0:T(8,128)(2,1)S(1)}, u32[]{:S(2)}, u32[]{:S(2)}) async-start(bf16[32,36,512]{2,1,0:T(8,128)(2,1)} %copy.142), calls=%async_computation.7 | async-start | bytes 2621440 | tf_op jit(solution)/shard_map/all_to_all | solution.py:79
Sparse Core Ops, SparseCore 0:
  10.6 101.7 all-gather.4
  115.5 95.3 all-gather.6
where the time goes:
time: 296 us; the launch traced here: 290 us
  waiting for transfers between devices  89.5 us (30%)
  local copies, waits for them, and re-layouts  68.9 us (23%)
  matrix products  58.9 us (20%)
  starting transfers between devices  38.9 us (13%)
  other arithmetic  19.1 us (6%)
  between operations  14.8 us (5%)
    dot_general x2, matrix products, local(): jnp.einsum('iqcsb,qsbe->iqcse', rounded, environ_k, preferred_element_typ...  38.3 us
    all_to_all x2, waiting for transfers between devices, local(): lax.all_to_all(send_rows, 'sector', split_axis=0, concat_axis=0, tiled=True)  34.2 us
    all_to_all x2, waiting for transfers between devices, local(): lax.all_to_all(advanced.reshape(sector_total, slot_count, block_width), '...  26.1 us
    all_gather x2, waiting for transfers between devices, local(): lax.all_gather(environments[orbital], 'section', axis=2, tiled=True)  25.2 us
    reshape x2, local copies, waits for them, and re-layouts, local(): amplitudes.reshape(sector_count, per_device, slot_count, OUTCOMES, block_...  23.9 us
    dot_general x2, matrix products, local(): jnp.einsum('iqcb,qbf->iqcf', arranged, site_k, preferred_element_type=jnp...  20.6 us
    reduce_sum x2, other arithmetic, branch_results(): picked = jnp.sum(chosen_mask[..., None] * amplitudes, axis=-2)  14.4 us
    reduce_sum x4, local copies, waits for them, and re-layouts, branch_results(): picked = jnp.sum(chosen_mask[..., None] * amplitudes, axis=-2)  12.3 us
  transfers between devices with their start and end apart: 10, of which 7 were waited for; matrix products, arithmetic and copies ran while one was open for 49% of the time, Pallas kernels for 0%

commit v1 on v0

--- a/solution.py
+++ b/solution.py
@@ -40,7 +40,11 @@
     current = vectors
     columns = []
     for orbital in range(ORBITALS):
-        environ_k = lax.all_gather(environments[orbital], "section", axis=2, tiled=True)
+        x = environments[orbital]
+        size = lax.axis_size("section")
+        blocks = jnp.stack([x for _ in range(size)])
+        blocks = lax.all_to_all(blocks, "section", split_axis=0, concat_axis=0)
+        environ_k = jnp.concatenate(blocks, axis=2)
         site_k = sites[orbital]
         labels = sectors[:, orbital]
         slot_of = labels * capacity + slot_positions(labels, sector_total)

time: 296 us -> 635 us (2.15)
  waiting for transfers between devices: 89.5 us -> 375 us
  local copies, waits for them, and re-layouts: 68.9 us -> 91.6 us
  blocking collectives: 0 us -> 22.5 us
  starting transfers between devices: 38.9 us -> 56.7 us
  between operations: 14.8 us -> 1.54 us
    all_to_all x0 -> x2, waiting for transfers between devices: none -> 332 us  [local(): blocks = lax.all_to_all(blocks, 'section', split_axis=0, concat_axis=0)]
    all_gather x2 -> x0, waiting for transfers between devices: 25.2 us -> none  [local(): lax.all_gather(environments[orbital], 'section', axis=2, tiled=True)]
    all_to_all x0 -> x2, starting transfers between devices: none -> 22.8 us  [local(): blocks = lax.all_to_all(blocks, 'section', split_axis=0, concat_axis=0)]
    all_to_all x0 -> x1, blocking collectives: none -> 22.5 us  [local(): lax.all_to_all(advanced.reshape(sector_total, slot_count, block_width), '...]
    reshape x0 -> x2, local copies, waits for them, and re-layouts: none -> 16.5 us  [local(): environ_k = jnp.concatenate(blocks, axis=2)]
    all_to_all x2 -> x1, waiting for transfers between devices: 26.1 us -> 13.2 us  [local(): lax.all_to_all(advanced.reshape(sector_total, slot_count, block_width), '...]
    another operation x1 -> x3, local copies, waits for them, and re-layouts: 0.22 us -> 8.87 us  [the longest x2 8.65 us: local(): blocks = jnp.stack([x for _ in range(size)])]
    all_to_all x2, waiting for transfers between devices: 34.2 us -> 26.3 us  [local(): lax.all_to_all(send_rows, 'sector', split_axis=0, concat_axis=0, tiled=True)]
  transfers between devices with their start and end apart: 10 -> 9, of which waited for: 7 -> 7; matrix products, arithmetic and copies ran while one was open for 49% -> 24% of each run, Pallas kernels for 0% -> 0%
where the time goes in v1:
time: 635 us; the launch traced here: 625 us
  waiting for transfers between devices  375 us (59%)
  local copies, waits for them, and re-layouts  91.6 us (14%)
  matrix products  58.5 us (9%)
  starting transfers between devices  56.7 us (9%)
  blocking collectives  22.5 us (4%)
  other arithmetic  19.2 us (3%)
    all_to_all x2, waiting for transfers between devices, local(): blocks = lax.all_to_all(blocks, 'section', split_axis=0, concat_axis=0)  332 us
    dot_general x2, matrix products, local(): jnp.einsum('iqcsb,qsbe->iqcse', rounded, environ_k, preferred_element_typ...  38 us
    all_to_all x2, waiting for transfers between devices, local(): lax.all_to_all(send_rows, 'sector', split_axis=0, concat_axis=0, tiled=True)  26.3 us
    reshape x2, local copies, waits for them, and re-layouts, local(): amplitudes.reshape(sector_count, per_device, slot_count, OUTCOMES, block_...  23.8 us
    all_to_all x2, starting transfers between devices, local(): blocks = lax.all_to_all(blocks, 'section', split_axis=0, concat_axis=0)  22.8 us
    all_to_all x1, blocking collectives, local(): lax.all_to_all(advanced.reshape(sector_total, slot_count, block_width), '...  22.5 us
    dot_general x2, matrix products, local(): jnp.einsum('iqcb,qbf->iqcf', arranged, site_k, preferred_element_type=jnp...  20.5 us
    reshape x2, local copies, waits for them, and re-layouts, local(): environ_k = jnp.concatenate(blocks, axis=2)  16.5 us
  transfers between devices with their start and end apart: 9, of which 7 were waited for; matrix products, arithmetic and copies ran while one was open for 24% of the time, Pallas kernels for 0%

profile of v1, /device:TPU:1, one launch (start us, length us, event | category | flops | bytes accessed | tf_op | source)
XLA Modules:
  0.0 625.0 jit_solution(16497449968998747494)
XLA Ops:
  4.2 3.0 scatter_custom_fusion.1
  7.8 6.5 %all-to-all-start.2 = ((bf16[8,4,36]{2,1,0:T(4,128)(2,1)}), bf16[8,4,36]{2,1,0:T(4,128)(2,1)S(1)}, u32[]{:S(2)}, u32[]{:S(2)}) async-start(bf16[8,4,36]{2,1,0:T(4,128)(2,1)} %all_to_all.38), calls=%async_computation.2 | async-start | bytes 16384 | tf_op jit(solution)/shard_map/all_to_all | solution.py:62
  19.0 4.2 all-to-all-start
  23.2 17.9 %all-to-all-done = bf16[32,36,512]{2,1,0:T(8,128)(2,1)S(1)} async-done(((bf16[32,36,512]{2,1,0:T(8,128)(2,1)}), bf16[32,36,512]{2,1,0:T(8,128)(2,1)S(1)}, u32[]{:S(2)}, u32[]{:S(2)}) %all-to-all-start) | async-done | bytes 1179680 | tf_op jit(solution)/shard_map/all_to_all | solution.py:61
  41.1 4.4 stack.6
  45.4 10.8 %all-to-all-start.1 = ((bf16[32,4,4,16,512]{4,3,2,1,0:T(8,128)(2,1)}), bf16[32,4,4,16,512]{4,3,2,1,0:T(8,128)(2,1)}, u32[]{:S(2)}, u32[]{:S(2)}) async-start(bf16[32,4,4,16,512]{4,3,2,1,0:T(8,128)(2,1)} %stack.6), calls=%async_computation.1 | async-start | bytes 16777216 | tf_op jit(solution)/shard_map/all_to_all | solution.py:46
  57.5 3.5 scatter_custom_fusion.3
  62.1 10.3 %fusion.10 = f32[8,4,36,2048]{3,2,0,1:T(8,128)} fusion(bf16[2,4,512,2048]{3,2,1,0:T(8,128)(2,1)} %param.8, bf16[8,4,36,512]{3,2,1,0:T(8,128)(2,1)S(1)} %bitcast.124), kind=kOutput, calls=%fused_computation.24 | convolution fusion | flops 2415919104 | bytes 19005440 | tf_op jit(solution)/shard_map/iqcb,qbf->iqcf/dot_general | solution.py:65
  72.4 11.9 %reshape.212 = f32[8,4,36,4,512]{4,3,2,0,1:T(4,128)} reshape(f32[8,4,36,2048]{3,2,0,1:T(8,128)} %fusion.10) | data formatting | bytes 18874368 | tf_op jit(solution)/shard_map/reshape | solution.py:68
  84.2 8.0 %multiply_reduce_fusion.1 = f32[8,4,36,512]{3,0,2,1:T(8,128)S(1)} fusion(f32[8,4,36,4,512]{4,3,2,0,1:T(4,128)} %reshape.212, f32[8,4,36,4]{3,0,2,1:T(8,128)S(1)} %copy.121), kind=kLoop, calls=%fused_computation.11 | loop fusion | flops 4128768 | bytes 11814912 | tf_op jit(solution)/shard_map/reduce_sum | solution.py:27
  92.2 3.5 copy.122
  98.4 147.3 %all-to-all-done.1 = bf16[32,4,4,16,512]{4,3,2,1,0:T(8,128)(2,1)} async-done(((bf16[32,4,4,16,512]{4,3,2,1,0:T(8,128)(2,1)}), bf16[32,4,4,16,512]{4,3,2,1,0:T(8,128)(2,1)}, u32[]{:S(2)}, u32[]{:S(2)}) %all-to-all-start.1) | async-done | bytes 8388640 | tf_op jit(solution)/shard_map/all_to_all | solution.py:46
  245.7 4.9 all-to-all-start.7
  250.6 8.2 %copy.111 = bf16[4,4,32,16,512]{4,3,2,1,0:T(8,128)(2,1)} copy(bf16[4,4,32,16,512]{4,3,1,0,2:T(8,128)(2,1)} %bitcast.7) | data formatting | bytes 16777216 | tf_op jit(solution)/shard_map/reshape | solution.py:47
  258.8 18.9 %fusion.16 = (f32[8,4,36]{2,0,1:T(8,128)S(1)}, f32[8,4,36,4]{2,0,3,1:T(8,128)S(1)}) fusion(f32[8,4,36,4,512]{4,3,2,0,1:T(4,128)} %reshape.212, bf16[4,4,512,512,1]{3,2,4,1,0:T(8,128)(2,1)} %bitcast.123), kind=kOutput, calls=%fused_computation.26 | convolution fusion | flops 2422991360 | bytes 17848832 | tf_op jit(solution)/shard_map/iqcsb,qsbe->iqcse/dot_general | solution.py:70
  278.8 22.5 %all_to_all.58 = bf16[32,36,512]{2,1,0:T(8,128)(2,1)S(1)} all-to-all(bf16[32,36,512]{2,1,0:T(8,128)(2,1)S(1)} %copy.127), channel_id=1, replica_groups=mesh['sector'=8,'section'=32] {'sector'}, dimensions={0} | all-to-all | bytes 2359296 | tf_op jit(solution)/shard_map/all_to_all | solution.py:83
  301.3 4.3 stack.7
  305.6 12.0 %all-to-all-start.6 = ((bf16[32,4,4,16,512]{4,3,2,1,0:T(8,128)(2,1)}), bf16[32,4,4,16,512]{4,3,2,1,0:T(8,128)(2,1)}, u32[]{:S(2)}, u32[]{:S(2)}) async-start(bf16[32,4,4,16,512]{4,3,2,1,0:T(8,128)(2,1)} %stack.7), calls=%async_computation.6 | async-start | bytes 16777216 | tf_op jit(solution)/shard_map/all_to_all | solution.py:46
  317.9 4.1 scatter_custom_fusion.2
  323.2 184.8 %all-to-all-done.6 = bf16[32,4,4,16,512]{4,3,2,1,0:T(8,128)(2,1)} async-done(((bf16[32,4,4,16,512]{4,3,2,1,0:T(8,128)(2,1)}), bf16[32,4,4,16,512]{4,3,2,1,0:T(8,128)(2,1)}, u32[]{:S(2)}, u32[]{:S(2)}) %all-to-all-start.6) | async-done | bytes 8388640 | tf_op jit(solution)/shard_map/all_to_all | solution.py:46
  508.0 4.9 all-to-all-start.5
  513.4 8.3 %copy.131 = bf16[4,4,32,16,512]{4,3,2,1,0:T(8,128)(2,1)} copy(bf16[4,4,32,16,512]{4,3,1,0,2:T(8,128)(2,1)} %bitcast.22) | data formatting | bytes 16777216 | tf_op jit(solution)/shard_map/reshape | solution.py:47
  522.4 8.5 %all-to-all-done.5 = bf16[32,36,512]{2,1,0:T(8,128)(2,1)S(1)} async-done(((bf16[32,36,512]{2,1,0:T(8,128)(2,1)}), bf16[32,36,512]{2,1,0:T(8,128)(2,1)S(1)}, u32[]{:S(2)}, u32[]{:S(2)}) %all-to-all-start.5) | async-done | bytes 1179680 | tf_op jit(solution)/shard_map/all_to_all | solution.py:61
  530.9 4.4 all-to-all-start.3
  535.2 10.3 %fusion.13 = f32[8,4,36,2048]{3,2,0,1:T(8,128)} fusion(bf16[2,4,512,2048]{3,2,1,0:T(8,128)(2,1)} %param.8, bf16[8,4,36,512]{3,2,1,0:T(8,128)(2,1)S(1)} %bitcast.125), kind=kOutput, calls=%fused_computation.25 | convolution fusion | flops 2415919104 | bytes 19005440 | tf_op jit(solution)/shard_map/iqcb,qbf->iqcf/dot_general | solution.py:65
  545.5 11.9 %reshape.213 = f32[8,4,36,4,512]{4,3,2,0,1:T(4,128)} reshape(f32[8,4,36,2048]{3,2,0,1:T(8,128)} %fusion.13) | data formatting | bytes 18874368 | tf_op jit(solution)/shard_map/reshape | solution.py:68
  557.4 19.1 %fusion.18 = (f32[8,4,36]{2,0,1:T(8,128)S(1)}, f32[8,4,36,4]{2,0,3,1:T(8,128)S(1)}) fusion(f32[8,4,36,4,512]{4,3,2,0,1:T(4,128)} %reshape.213, bf16[4,4,512,512,1]{3,2,4,1,0:T(8,128)(2,1)} %bitcast.122), kind=kOutput, calls=%fused_computation.28 | convolution fusion | flops 2422991360 | bytes 17848832 | tf_op jit(solution)/shard_map/iqcsb,qsbe->iqcse/dot_general | solution.py:70
  576.6 6.4 %multiply_reduce_fusion = f32[8,4,36,512]{3,0,2,1:T(8,128)S(1)} fusion(f32[8,4,36,4,512]{4,3,2,0,1:T(4,128)S(1)} %bitcast.121, f32[8,4,36,4]{3,0,2,1:T(8,128)S(1)} %copy.142), kind=kLoop, calls=%fused_computation.10 | loop fusion | flops 4128768 | bytes 11814912 | tf_op jit(solution)/shard_map/reduce_sum | solution.py:27
  583.2 3.5 copy.143
  590.1 4.8 all-to-all-start.8
  599.5 4.2 all-to-all-start.9
  608.4 13.2 %all-to-all-done.9 = bf16[32,36,512]{2,1,0:T(8,128)(2,1)S(1)} async-done(((bf16[32,36,512]{2,1,0:T(8,128)(2,1)}), bf16[32,36,512]{2,1,0:T(8,128)(2,1)S(1)}, u32[]{:S(2)}, u32[]{:S(2)}) %all-to-all-start.9) | async-done | bytes 1179680 | tf_op jit(solution)/shard_map/all_to_all | solution.py:83
  (84 shorter events, 33.3 us)
Async XLA Ops:
  0.6 22.5 %copy-start = (bf16[2,4,4,16,512]{4,3,2,1,0:T(8,128)(2,1)S(1)}, bf16[2,4,4,16,512]{4,3,2,1,0:T(8,128)(2,1)}, u32[]{:S(2)}) copy-start(bf16[2,4,4,16,512]{4,3,2,1,0:T(8,128)(2,1)} %param.9) | copy-start | bytes 1572868
  7.8 11.1 %all-to-all-start.2 = ((bf16[8,4,36]{2,1,0:T(4,128)(2,1)}), bf16[8,4,36]{2,1,0:T(4,128)(2,1)S(1)}, u32[]{:S(2)}, u32[]{:S(2)}) async-start(bf16[8,4,36]{2,1,0:T(4,128)(2,1)} %all_to_all.38), calls=%async_computation.2 | async-start | bytes 16384 | tf_op jit(solution)/shard_map/all_to_all | solution.py:62
  19.0 22.1 %all-to-all-start = ((bf16[32,36,512]{2,1,0:T(8,128)(2,1)}), bf16[32,36,512]{2,1,0:T(8,128)(2,1)S(1)}, u32[]{:S(2)}, u32[]{:S(2)}) async-start(bf16[32,36,512]{2,1,0:T(8,128)(2,1)} %reshape.129), calls=%async_computation | async-start | bytes 2621440 | tf_op jit(solution)/shard_map/all_to_all | solution.py:61
  45.4 12.0 %copy-start.1 = (s32[384,2]{0,1:T(2,128)S(1)}, s32[384,2]{0,1:T(2,128)}, u32[]{:S(2)}) copy-start(s32[384,2]{0,1:T(2,128)} %param.6) | copy-start | bytes 9220
  45.4 200.3 %all-to-all-start.1 = ((bf16[32,4,4,16,512]{4,3,2,1,0:T(8,128)(2,1)}), bf16[32,4,4,16,512]{4,3,2,1,0:T(8,128)(2,1)}, u32[]{:S(2)}, u32[]{:S(2)}) async-start(bf16[32,4,4,16,512]{4,3,2,1,0:T(8,128)(2,1)} %stack.6), calls=%async_computation.1 | async-start | bytes 16777216 | tf_op jit(solution)/shard_map/all_to_all | solution.py:46
  245.7 33.1 %all-to-all-start.7 = ((bf16[8,4,36]{2,1,0:T(4,128)(2,1)}), bf16[8,4,36]{2,1,0:T(4,128)(2,1)S(1)}, u32[]{:S(2)}, u32[]{:S(2)}) async-start(bf16[8,4,36]{2,1,0:T(4,128)(2,1)} %all_to_all.44), calls=%async_computation.7 | async-start | bytes 16384 | tf_op jit(solution)/shard_map/all_to_all | solution.py:62
  305.6 202.4 %all-to-all-start.6 = ((bf16[32,4,4,16,512]{4,3,2,1,0:T(8,128)(2,1)}), bf16[32,4,4,16,512]{4,3,2,1,0:T(8,128)(2,1)}, u32[]{:S(2)}, u32[]{:S(2)}) async-start(bf16[32,4,4,16,512]{4,3,2,1,0:T(8,128)(2,1)} %stack.7), calls=%async_computation.6 | async-start | bytes 16777216 | tf_op jit(solution)/shard_map/all_to_all | solution.py:46
  508.0 22.9 %all-to-all-start.5 = ((bf16[32,36,512]{2,1,0:T(8,128)(2,1)}), bf16[32,36,512]{2,1,0:T(8,128)(2,1)S(1)}, u32[]{:S(2)}, u32[]{:S(2)}) async-start(bf16[32,36,512]{2,1,0:T(8,128)(2,1)} %reshape.137), calls=%async_computation.5 | async-start | bytes 2621440 | tf_op jit(solution)/shard_map/all_to_all | solution.py:61
  530.9 59.2 %all-to-all-start.3 = ((bf16[8,2,288]{2,1,0:T(2,128)(2,1)}), bf16[8,2,288]{2,1,0:T(2,128)(2,1)S(1)}, u32[]{:S(2)}, u32[]{:S(2)}) async-start(bf16[8,2,288]{2,1,0:T(2,128)(2,1)} %reshape.238), calls=%async_computation.3 | async-start | bytes 24576 | tf_op jit(solution)/shard_map/all_to_all | solution.py:76
  557.4 19.2 %slice-start = ((s8[9437184]{0:T(1024)(128)(4,1)}), s8[4194304]{0:T(1024)(128)(4,1)S(1)}, s32[]{:S(2)}) async-start(s8[9437184]{0:T(1024)(128)(4,1)} %bitcast.120), calls=%async_computation.10 | async-start | bytes 8388608
  557.4 19.2 %slice-start.1 = ((s8[9437184]{0:T(1024)(128)(4,1)}), s8[4194304]{0:T(1024)(128)(4,1)S(1)}, s32[]{:S(2)}) async-start(s8[9437184]{0:T(1024)(128)(4,1)} %bitcast.120), calls=%async_computation.11 | async-start | bytes 8388608
  557.4 19.2 %slice-start.2 = ((s8[9437184]{0:T(1024)(128)(4,1)}), s8[1048576]{0:T(1024)(128)(4,1)S(1)}, s32[]{:S(2)}) async-start(s8[9437184]{0:T(1024)(128)(4,1)} %bitcast.120), calls=%async_computation.12 | async-start | bytes 2097152
  590.1 9.5 %all-to-all-start.8 = ((bf16[8,2,288]{2,1,0:T(2,128)(2,1)}), bf16[8,2,288]{2,1,0:T(2,128)(2,1)S(1)}, u32[]{:S(2)}, u32[]{:S(2)}) async-start(bf16[8,2,288]{2,1,0:T(2,128)(2,1)} %reshape.236), calls=%async_computation.8 | async-start | bytes 24576 | tf_op jit(solution)/shard_map/all_to_all | solution.py:76
  599.5 22.1 %all-to-all-start.9 = ((bf16[32,36,512]{2,1,0:T(8,128)(2,1)}), bf16[32,36,512]{2,1,0:T(8,128)(2,1)S(1)}, u32[]{:S(2)}, u32[]{:S(2)}) async-start(bf16[32,36,512]{2,1,0:T(8,128)(2,1)} %copy.148), calls=%async_computation.9 | async-start | bytes 2621440 | tf_op jit(solution)/shard_map/all_to_all | solution.py:83
